TPU v7x, 256 devices: a whole 4x4x8 slice. The times are simulated.
256 devices in a mesh: shard: 64 (over z, y, core), help: 4 (over x).
Axes of the slice: x: 4, y: 4, z: 8, core: 2. Of those that a mesh axis runs over, the one named last changes fastest.
Arguments:
- queries: bfloat16 [65536, 768], P(('shard', 'help')), may hold values from -6 to 6
- probe_group: int32 [65536, 2], P(('shard', 'help')), may hold values from 0 to 63, all different within a row; in each aligned block of 256 rows (0 to 255, 256 to 511, ...) at most 16 rows name the same one
- probe_local: int32 [65536, 2], P(('shard', 'help')), may hold values from 0 to 3
- points: bfloat16 [262144, 768], P(('shard', 'help')), may hold values from -6 to 6
- point_cluster: int32 [64, 4096], P('shard'), may hold values from 0 to 3, never falling along the last dimension, each value on 1 to 3072 neighbouring positions
- test_matrix: bfloat16 [32, 262144], P(None, ('shard', 'help')), may hold values from -6 to 6
Outputs:
- sketch: float32 [32, 262144], P(None, ('shard', 'help'))
- regressor: float32 [256, 32, 768], P(('shard', 'help'))
Inputs may be any that keep to these rules, and one draw needn't show every extreme that they name: `probe_group`: A query's 2 groups differ. Among the 256 queries of one device (aligned blocks of rows), at most 16 pairs (q,k) name one group, and in some blocks one group is named exactly 16 times.
All inputs are finite; a program needn't handle non-finite values.
Results may differ from a plain program's by a relative error of at most 0.0037.
Values may be sent and summed in bfloat16 or wider, within the bound.
A program may use at most 64 MiB of HBM per device.

v0:
```python
import jax
import jax.numpy as jnp
from jax import lax
from jax.sharding import PartitionSpec as P

PROBES = 2
CL_DEV = 1


def masked_scores(point_rows, point_ids, query_rows, query_ids):
    feature_width = point_rows.shape[1]
    block_rows = min(512, point_rows.shape[0])
    factor = feature_width ** (-0.5)

    def score_piece(pieces):
        piece_x, piece_ids = pieces
        product = (
            lax.dot_general(
                piece_x, query_rows, (((1,), (1,)), ((), ())), preferred_element_type=jnp.float32
            )
            * factor
        )
        return jnp.where(piece_ids[:, None] == query_ids[None, :], product, 0.0).astype(
            jnp.bfloat16
        )

    stacked = lax.map(
        score_piece,
        (point_rows.reshape(-1, block_rows, feature_width), point_ids.reshape(-1, block_rows)),
    )
    return stacked.reshape(point_rows.shape[0], query_rows.shape[0])


def pack_rows(source, target, member, groups, blocks, capacity, probes):
    feature_width = source.shape[1]
    row_total = target.shape[0]
    per_block = row_total // blocks
    labels = jnp.arange(groups, dtype=jnp.int32)
    onehot_dest = (
        (target[:, None] == labels[None, :]).astype(jnp.int32).reshape(blocks, per_block, groups)
    )
    ranking = jnp.sum((jnp.cumsum(onehot_dest, axis=1) - onehot_dest) * onehot_dest, axis=2)
    position = (
        target.reshape(blocks, per_block) * (blocks * capacity)
        + jnp.arange(blocks, dtype=jnp.int32)[:, None] * capacity
        + ranking
    )
    position = position.reshape(-1)
    copied_rows = jnp.repeat(source, probes, axis=0)
    filled = (
        jnp.zeros((groups * blocks * capacity, feature_width), jnp.bfloat16)
        .at[position]
        .set(copied_rows)
    )
    labelled = jnp.full((groups * blocks * capacity,), -1, jnp.int32).at[position].set(member)
    return (
        filled.reshape(groups, blocks * capacity, feature_width),
        labelled.reshape(groups, blocks * capacity),
    )


def count_labels(ids, labels):
    return jnp.sum((ids[None, :] == labels[:, None]).astype(jnp.float32), axis=1)


def shards(queries, probe_group, probe_local, points, point_cluster, test_matrix):
    groups = lax.axis_size("shard")
    helpers = lax.axis_size("help")
    helper = lax.axis_index("help")
    feature_width = queries.shape[1]
    per_device = queries.shape[0] * PROBES
    capacity = 2 * per_device // groups
    group_clusters = CL_DEV * helpers
    own_points = points.shape[0]
    group_ids = point_cluster[0]
    own_ids = lax.dynamic_slice_in_dim(group_ids, helper * own_points, own_points, 0)
    labels = jnp.arange(group_clusters, dtype=jnp.int32)
    resident = count_labels(group_ids, labels)
    peer_rows, peer_groups, peer_local = (
        lax.all_gather(queries, "help", axis=0, tiled=True),
        lax.all_gather(probe_group, "help", axis=0, tiled=True),
        lax.all_gather(probe_local, "help", axis=0, tiled=True),
    )
    outgoing, out_ids = pack_rows(
        peer_rows,
        peer_groups.reshape(-1),
        peer_local.reshape(-1),
        groups,
        helpers,
        capacity,
        PROBES,
    )
    query_pool, pool_ids = (
        lax.all_to_all(outgoing, "shard", split_axis=0, concat_axis=0, tiled=True),
        lax.all_to_all(out_ids, "shard", split_axis=0, concat_axis=0, tiled=True),
    )
    query_rows = query_pool.reshape(-1, feature_width)
    query_ids = pool_ids.reshape(-1)
    scores = masked_scores(points, own_ids, query_rows, query_ids)
    lifted = lax.psum(
        jnp.dot(test_matrix, scores, preferred_element_type=jnp.float32), "help"
    ).astype(jnp.bfloat16)
    product = lax.dot_general(
        lifted, scores, (((1,), (1,)), ((), ())), preferred_element_type=jnp.float32
    )
    queried = count_labels(query_ids, labels)
    factor = 1.0 / jnp.sqrt((queried + 1.0) * (queried + resident))
    own_hot = (own_ids[None, :] == labels[:, None]).astype(jnp.float32)
    sketch = product * jnp.sum(factor[:, None] * own_hot, axis=0)[None, :]
    rounded = sketch.astype(jnp.bfloat16)
    hot_rows = own_hot.astype(jnp.bfloat16)
    weighted = (hot_rows[:, None, :] * rounded[None, :, :]).reshape(
        CL_DEV * lax.axis_size("help") * rounded.shape[0], own_points
    )
    summed = jnp.dot(weighted, points, preferred_element_type=jnp.float32)
    partial_sum = lax.psum_scatter(
        summed.reshape(CL_DEV * lax.axis_size("help"), rounded.shape[0], feature_width),
        "help",
        scatter_dimension=0,
        tiled=True,
    )
    scale_own = lax.dynamic_slice_in_dim(1.0 / jnp.sqrt(resident), helper * CL_DEV, CL_DEV, 0)
    regressor = partial_sum * scale_own[:, None, None]
    return (sketch, regressor)


def solution(mesh):
    in_specs = (
        P(("shard", "help"), None),
        P(("shard", "help"), None),
        P(("shard", "help"), None),
        P(("shard", "help"), None),
        P("shard", None),
        P(None, ("shard", "help")),
    )
    out_specs = (P(None, ("shard", "help")), P(("shard", "help"), None, None))
    return jax.shard_map(shards, mesh=mesh, in_specs=in_specs, out_specs=out_specs, check_vma=False)
```

profile of v0, /device:TPU:8, one launch (start us, length us, event | category | flops | bytes accessed | tf_op | source)
XLA Modules:
  0.0 307.3 jit_solution(3238835004986476215)
XLA Ops:
  7.2 0.7 all-gather.2.cloned.1.call-update
  7.9 11.3 %all_gather.9 = s32[1024,2]{0,1:T(2,128)S(1)} all-gather(s32[256,2]{0,1:T(2,128)} %param.9), channel_id=1, replica_groups=mesh['shard'=64,'help'=4] {'help'}, dimensions={0}, use_global_device_ids=true | all-gather | bytes 10240 | tf_op jit(solution)/shard_map/all_gather | solution.py:81
  20.1 4.8 %reduce-window.6 = s32[4,64,4,128]{3,1,2,0:T(8,128)S(1)} reduce-window(s32[4,64,4,128]{3,1,2,0:T(8,128)S(1)} %fusion.12, s32[]{:T(128)} %constant.9.clone.1), window={size=1x1x1x128 pad=0_0x0_0x0_0x127_0}, to_apply=%region_0.0 | reduce-window | flops 16646144 | bytes 1048580 | tf_op jit(solution)/shard_map/reduce-window
  26.4 10.8 %all_gather.10 = s32[1024,2]{0,1:T(2,128)S(1)} all-gather(s32[256,2]{0,1:T(2,128)} %param.10), channel_id=1, replica_groups=mesh['shard'=64,'help'=4] {'help'}, dimensions={0}, use_global_device_ids=true | all-gather | bytes 10240 | tf_op jit(solution)/shard_map/all_gather | solution.py:82
  37.7 8.1 %scatter_custom_fusion = s32[4096]{0:T(1024)S(1)} fusion(s32[2048]{0:T(1024)S(1)} %bitcast.81, s32[2048]{0:T(1024)S(1)} %reshape.158, s32[]{:T(128)} %constant.20.clone.1), kind=kCustom, calls=%fused_computation.37 | custom fusion | bytes 16388 | tf_op jit(solution)/shard_map/scatter | solution.py:55
  45.7 0.7 all_to_all.11
  46.4 12.1 %all-to-all-start = ((s32[64,1,64]{2,1,0:T(1,128)}), s32[64,1,64]{2,1,0:T(1,128)S(1)}, u32[]{:S(2)}, u32[]{:S(2)}) async-start(s32[64,1,64]{2,1,0:T(1,128)} %all_to_all.11), calls=%async_computation | async-start | bytes 65536 | tf_op jit(solution)/shard_map/all_to_all | solution.py:95
  58.6 3.0 broadcast_in_dim.20
  61.6 2.7 reshape.166
  64.3 13.9 %scatter_custom_fusion.1 = bf16[4096,768]{1,0:T(8,128)(2,1)} fusion(s32[2048]{0:T(1024)S(1)} %bitcast.82, bf16[2048,768]{1,0:T(8,128)(2,1)} %reshape.166, bf16[]{:T(256)} %constant.22.clone.1), kind=kCustom, calls=%fused_computation.10 | custom fusion | bytes 6291968 | tf_op jit(solution)/shard_map/scatter | solution.py:53
  78.2 10.6 %all-to-all-start.1 = ((bf16[64,64,768]{2,1,0:T(8,128)(2,1)}), bf16[64,64,768]{2,1,0:T(8,128)(2,1)}, u32[]{:S(2)}, u32[]{:S(2)}) async-start(bf16[64,64,768]{2,1,0:T(8,128)(2,1)} %bitcast.69), calls=%async_computation.1 | async-start | bytes 12582912 | tf_op jit(solution)/shard_map/all_to_all | solution.py:94
  89.4 0.7 fusion.19
  90.2 0.7 reduce.9
  91.3 138.7 %all-to-all-done.1 = bf16[64,64,768]{2,1,0:T(8,128)(2,1)} async-done(((bf16[64,64,768]{2,1,0:T(8,128)(2,1)}), bf16[64,64,768]{2,1,0:T(8,128)(2,1)}, u32[]{:S(2)}, u32[]{:S(2)}) %all-to-all-start.1) | async-done | bytes 6291488 | tf_op jit(solution)/shard_map/all_to_all | solution.py:94
  230.0 15.6 %while.11 = (s32[]{:T(128)}, bf16[2,512,4096]{2,1,0:T(8,128)(2,1)}, s32[2,512]{1,0:T(2,128)S(1)}, s32[64,64]{1,0:T(8,128)}, bf16[2,512,768]{2,1,0:T(8,128)(2,1)S...) while((s32[]{:T(128)}, bf16[2,512,4096]{2,1,0:T(8,128)(2,1)}, ...), condition=%wide.wide.region_6.7_spmd, body=%wide.wide.region_5.6_spmd.sunk | while | flops 3229614080 | bytes 11295833 | solution.py:27
  230.0 7.8 %fusion.35 = bf16[2,512,4096]{2,1,0:T(8,128)(2,1)} fusion(bf16[2,512,4096]{2,1,0:T(8,128)(2,1)} %get-tuple-element.131, s32[]{:T(128)} %get-tuple-element.130, bf16[4096,768]{1,0:T(8,128)(2,1)} %get-tuple-element.143, s32[4096]{0:T(1024)S(1)} %get-tuple-element.144, s32[512]{0:T(512)S(1)} %bitcast.74, ...), kind=kOutput, calls=%fused_computation.4.clone.clone.1 | convolution fusion | flops 3229614080 | bytes 11291648 | tf_op jit(solution)/shard_map/while/body/eval_jaxpr/dot_general | solution.py:18
  237.8 7.8 %fusion.35 = bf16[2,512,4096]{2,1,0:T(8,128)(2,1)} fusion(bf16[2,512,4096]{2,1,0:T(8,128)(2,1)} %get-tuple-element.131, s32[]{:T(128)} %get-tuple-element.130, bf16[4096,768]{1,0:T(8,128)(2,1)} %get-tuple-element.143, s32[4096]{0:T(1024)S(1)} %get-tuple-element.144, s32[512]{0:T(512)S(1)} %bitcast.74, ...), kind=kOutput, calls=%fused_computation.4.clone.clone.1 | convolution fusion | flops 3229614080 | bytes 11291648 | tf_op jit(solution)/shard_map/while/body/eval_jaxpr/dot_general | solution.py:18
  245.6 4.9 %convolution_bitcast_fusion = f32[32,4096]{1,0:T(8,128)S(1)} fusion(bf16[32,1024]{1,0:T(8,128)(2,1)S(1)} %copy-done, bf16[1024,4096]{1,0:T(8,128)(2,1)} %bitcast.67), kind=kOutput, calls=%fused_computation.9 | convolution fusion | flops 268435456 | bytes 8978432 | tf_op jit(solution)/shard_map/dot_general | solution.py:101
  250.5 21.6 %all-reduce.1 = bf16[32,4096]{1,0:T(8,128)(2,1)S(1)} all-reduce(f32[32,4096]{1,0:T(8,128)S(1)} %convolution_bitcast_fusion), channel_id=1, replica_groups=mesh['shard'=64,'help'=4] {'help'}, use_global_device_ids=true, to_apply=%region_7.8 | all-reduce | flops 131072 | bytes 786432 | tf_op jit(solution)/shard_map/psum | solution.py:100
  272.1 6.6 %fusion.21 = (bf16[32,1024]{1,0:T(8,128)(2,1)S(1)}, f32[32,1024]{1,0:T(8,128)}) fusion(f32[1024]{0:T(1024)S(1)} %select_reduce_fusion, bf16[32,4096]{1,0:T(8,128)(2,1)S(1)} %all-reduce.1, bf16[1024,4096]{1,0:T(8,128)(2,1)} %bitcast.68), kind=kOutput, calls=%fused_computation.46 | convolution fusion | flops 268500992 | bytes 8851456 | tf_op jit(solution)/shard_map/dot_general | solution.py:103
  278.7 1.1 fusion.7
  279.9 0.6 dynamic_slice.15
  280.5 17.8 %reduce-scatter.2.cloned.1.call-done = f32[1,32,768]{2,1,0:T(8,128)} async-done(((f32[4,32,768]{2,1,0:T(8,128)}), f32[1,32,768]{2,1,0:T(8,128)}) %reduce-scatter.2.cloned.1.call-update) | async-done | bytes 98320 | tf_op jit(solution)/shard_map/reduce_scatter | solution.py:116
  298.3 2.2 broadcast_multiply_fusion
  (42 shorter events, 3.9 us)
Async XLA Ops:
  7.2 238.4 %copy-start = (bf16[32,1024]{1,0:T(8,128)(2,1)S(1)}, bf16[32,1024]{1,0:T(8,128)(2,1)}, u32[]{:S(2)}) copy-start(bf16[32,1024]{1,0:T(8,128)(2,1)} %param.13) | copy-start | bytes 196612
  7.2 51.4 %all-gather.2.cloned.1.call-start = ((), (), s32[]{:S(2)}) async-start(), calls=%async_computation.3 | async-start | bytes 1966080 | tf_op jit(solution)/shard_map/all_gather | solution.py:80
  46.4 31.8 %all-to-all-start = ((s32[64,1,64]{2,1,0:T(1,128)}), s32[64,1,64]{2,1,0:T(1,128)S(1)}, u32[]{:S(2)}, u32[]{:S(2)}) async-start(s32[64,1,64]{2,1,0:T(1,128)} %all_to_all.11), calls=%async_computation | async-start | bytes 65536 | tf_op jit(solution)/shard_map/all_to_all | solution.py:95
  78.2 12.0 %copy-start.2 = (s32[64,1,64]{2,1,0:T(1,128)}, s32[64,1,64]{2,1,0:T(1,128)S(1)}, u32[]{:S(2)}) copy-start(s32[64,1,64]{2,1,0:T(1,128)S(1)} %all-to-all-done) | copy-start | bytes 49156
  78.2 11.2 %copy-start.3 = (s32[1,4096]{1,0:T(1,128)S(1)}, s32[1,4096]{1,0:T(1,128)}, u32[]{:S(2)}) copy-start(s32[1,4096]{1,0:T(1,128)} %param.12) | copy-start | bytes 49156
  78.2 151.7 %copy-start.1 = (bf16[1024,768]{1,0:T(8,128)(2,1)S(1)}, bf16[1024,768]{1,0:T(8,128)(2,1)}, u32[]{:S(2)}) copy-start(bf16[1024,768]{1,0:T(8,128)(2,1)} %param.11) | copy-start | bytes 4718596
  78.2 151.7 %all-to-all-start.1 = ((bf16[64,64,768]{2,1,0:T(8,128)(2,1)}), bf16[64,64,768]{2,1,0:T(8,128)(2,1)}, u32[]{:S(2)}, u32[]{:S(2)}) async-start(bf16[64,64,768]{2,1,0:T(8,128)(2,1)} %bitcast.69), calls=%async_computation.1 | async-start | bytes 12582912 | tf_op jit(solution)/shard_map/all_to_all | solution.py:94
  88.8 209.5 %reduce-scatter.2.cloned.1.call-start = ((), (), s32[]{:S(2)}) async-start(), calls=%async_computation.4 | async-start | bytes 491520 | tf_op jit(solution)/shard_map/reduce_scatter | solution.py:116
Sparse Core Ops, SparseCore 0:
  9.8 31.9 all-gather.1
  280.0 18.2 reduce-scatter.1
where the time goes:
time: 308 us; the launch traced here: 307 us
  waiting for transfers between devices  157 us (51%)
  blocking collectives  43.6 us (14%)
  local copies, waits for them, and re-layouts  32.8 us (11%)
  matrix products  28.3 us (9%)
  starting transfers between devices  22.8 us (7%)
  between operations  14.2 us (5%)
  other arithmetic  8.3 us (3%)
    all_to_all x1, waiting for transfers between devices, shards(): lax.all_to_all(outgoing, 'shard', split_axis=0, concat_axis=0, tiled=True)  139 us
    psum x1, blocking collectives, shards(): lax.psum(jnp.dot(test_matrix, scores, preferred_element_type=jnp.float32)...  21.6 us
    reduce_scatter x1, waiting for transfers between devices, shards(): lax.psum_scatter(summed.reshape(CL_DEV * lax.axis_size('help'), rounded.s...  17.8 us
    dot_general x2, matrix products, score_piece(): lax.dot_general(piece_x, query_rows, (((1,), (1,)), ((), ())), preferred_...  15.6 us
    scatter x1, local copies, waits for them, and re-layouts, pack_rows(): filled = jnp.zeros((groups * blocks * capacity, feature_width), jnp.bfloa...  13.9 us
    all_to_all x1, starting transfers between devices, shards(): lax.all_to_all(out_ids, 'shard', split_axis=0, concat_axis=0, tiled=True)  12.1 us
    all_gather x1, blocking collectives, shards(): lax.all_gather(probe_group, 'help', axis=0, tiled=True)  11.3 us
    all_gather x1, blocking collectives, shards(): lax.all_gather(probe_local, 'help', axis=0, tiled=True)  10.8 us
  transfers between devices with their start and end apart: 4, of which 2 were waited for; matrix products, arithmetic and copies ran while one was open for 12% of the time, Pallas kernels for 0%

commit v1 on v0

--- a/solution.py
+++ b/solution.py
@@ -97,8 +97,9 @@
     query_rows = query_pool.reshape(-1, feature_width)
     query_ids = pool_ids.reshape(-1)
     scores = masked_scores(points, own_ids, query_rows, query_ids)
-    lifted = lax.psum(
-        jnp.dot(test_matrix, scores, preferred_element_type=jnp.float32), "help"
+    lifted = jnp.sum(
+        lax.all_gather(jnp.dot(test_matrix, scores, preferred_element_type=jnp.float32), "help"),
+        axis=0,
     ).astype(jnp.bfloat16)
     product = lax.dot_general(
         lifted, scores, (((1,), (1,)), ((), ())), preferred_element_type=jnp.float32

time: 308 us -> 323 us (1.049)
  waiting for transfers between devices: 157 us -> 192 us
  blocking collectives: 43.6 us -> 22.1 us
    all_gather x0 -> x1, waiting for transfers between devices: none -> 28.2 us  [shards(): lax.all_gather(jnp.dot(test_matrix, scores, preferred_element_type=jnp.fl...]
    psum x1 -> x0, blocking collectives: 21.6 us -> none  [shards(): lax.psum(jnp.dot(test_matrix, scores, preferred_element_type=jnp.float32)...]
    reduce_scatter x1, waiting for transfers between devices: 17.8 us -> 23.3 us  [shards(): lax.psum_scatter(summed.reshape(CL_DEV * lax.axis_size('help'), rounded.s...]
  transfers between devices with their start and end apart: 4 -> 5, of which waited for: 2 -> 3; matrix products, arithmetic and copies ran while one was open for 12% -> 12% of each run, Pallas kernels for 0% -> 0%
where the time goes in v1:
time: 323 us
  waiting for transfers between devices  192 us (59%)
  local copies, waits for them, and re-layouts  32.8 us (10%)
  matrix products  29.1 us (9%)
  starting transfers between devices  22.8 us (7%)
  blocking collectives  22.1 us (7%)
  between operations  14 us (4%)
  other arithmetic  10 us (3%)
    all_to_all x1, waiting for transfers between devices, shards(): lax.all_to_all(outgoing, 'shard', split_axis=0, concat_axis=0, tiled=True)  140 us
    all_gather x1, waiting for transfers between devices, shards(): lax.all_gather(jnp.dot(test_matrix, scores, preferred_element_type=jnp.fl...  28.2 us
    reduce_scatter x1, waiting for transfers between devices, shards(): lax.psum_scatter(summed.reshape(CL_DEV * lax.axis_size('help'), rounded.s...  23.3 us
    dot_general x2, matrix products, score_piece(): lax.dot_general(piece_x, query_rows, (((1,), (1,)), ((), ())), preferred_...  15.6 us
    scatter x1, local copies, waits for them, and re-layouts, pack_rows(): filled = jnp.zeros((groups * blocks * capacity, feature_width), jnp.bfloa...  13.9 us
    all_to_all x1, starting transfers between devices, shards(): lax.all_to_all(out_ids, 'shard', split_axis=0, concat_axis=0, tiled=True)  12.1 us
    all_gather x1, blocking collectives, shards(): lax.all_gather(probe_group, 'help', axis=0, tiled=True)  11.3 us
    all_gather x1, blocking collectives, shards(): lax.all_gather(probe_local, 'help', axis=0, tiled=True)  10.8 us
  transfers between devices with their start and end apart: 5, of which 3 were waited for; matrix products, arithmetic and copies ran while one was open for 12% of the time, Pallas kernels for 0%

profile of v1, /device:TPU:8, one launch (start us, length us, event | category | flops | bytes accessed | tf_op | source)
XLA Modules:
  0.0 322.9 jit_solution(7179414293531003438)
XLA Ops:
  7.2 0.7 all-gather.4.cloned.1.call-update
  7.9 11.3 %all_gather.15 = s32[1024,2]{0,1:T(2,128)S(1)} all-gather(s32[256,2]{0,1:T(2,128)} %param.9), channel_id=1, replica_groups=mesh['shard'=64,'help'=4] {'help'}, dimensions={0}, use_global_device_ids=true | all-gather | bytes 10240 | tf_op jit(solution)/shard_map/all_gather | solution.py:81
  20.1 4.8 %reduce-window.6 = s32[4,64,4,128]{3,1,2,0:T(8,128)S(1)} reduce-window(s32[4,64,4,128]{3,1,2,0:T(8,128)S(1)} %fusion.12, s32[]{:T(128)} %constant.9.clone.1), window={size=1x1x1x128 pad=0_0x0_0x0_0x127_0}, to_apply=%region_0.0 | reduce-window | flops 16646144 | bytes 1048580 | tf_op jit(solution)/shard_map/reduce-window
  26.4 10.8 %all_gather.16 = s32[1024,2]{0,1:T(2,128)S(1)} all-gather(s32[256,2]{0,1:T(2,128)} %param.10), channel_id=1, replica_groups=mesh['shard'=64,'help'=4] {'help'}, dimensions={0}, use_global_device_ids=true | all-gather | bytes 10240 | tf_op jit(solution)/shard_map/all_gather | solution.py:82
  37.7 8.1 %scatter_custom_fusion = s32[4096]{0:T(1024)S(1)} fusion(s32[2048]{0:T(1024)S(1)} %bitcast.84, s32[2048]{0:T(1024)S(1)} %reshape.158, s32[]{:T(128)} %constant.20.clone.1), kind=kCustom, calls=%fused_computation.37 | custom fusion | bytes 16388 | tf_op jit(solution)/shard_map/scatter | solution.py:55
  45.7 0.7 all_to_all.11
  46.4 12.1 %all-to-all-start = ((s32[64,1,64]{2,1,0:T(1,128)}), s32[64,1,64]{2,1,0:T(1,128)S(1)}, u32[]{:S(2)}, u32[]{:S(2)}) async-start(s32[64,1,64]{2,1,0:T(1,128)} %all_to_all.11), calls=%async_computation | async-start | bytes 65536 | tf_op jit(solution)/shard_map/all_to_all | solution.py:95
  58.6 3.0 broadcast_in_dim.20
  61.6 2.7 reshape.166
  64.3 13.9 %scatter_custom_fusion.1 = bf16[4096,768]{1,0:T(8,128)(2,1)} fusion(s32[2048]{0:T(1024)S(1)} %bitcast.85, bf16[2048,768]{1,0:T(8,128)(2,1)} %reshape.166, bf16[]{:T(256)} %constant.22.clone.1), kind=kCustom, calls=%fused_computation.10 | custom fusion | bytes 6291968 | tf_op jit(solution)/shard_map/scatter | solution.py:53
  78.2 10.6 %all-to-all-start.1 = ((bf16[64,64,768]{2,1,0:T(8,128)(2,1)}), bf16[64,64,768]{2,1,0:T(8,128)(2,1)}, u32[]{:S(2)}, u32[]{:S(2)}) async-start(bf16[64,64,768]{2,1,0:T(8,128)(2,1)} %bitcast.70), calls=%async_computation.1 | async-start | bytes 12582912 | tf_op jit(solution)/shard_map/all_to_all | solution.py:94
  89.5 0.6 fusion.19
  90.2 139.8 %all-to-all-done.1 = bf16[64,64,768]{2,1,0:T(8,128)(2,1)} async-done(((bf16[64,64,768]{2,1,0:T(8,128)(2,1)}), bf16[64,64,768]{2,1,0:T(8,128)(2,1)}, u32[]{:S(2)}, u32[]{:S(2)}) %all-to-all-start.1) | async-done | bytes 6291488 | tf_op jit(solution)/shard_map/all_to_all | solution.py:94
  230.0 15.6 %while.11 = (s32[]{:T(128)}, bf16[2,512,4096]{2,1,0:T(8,128)(2,1)}, s32[2,512]{1,0:T(2,128)S(1)}, s32[64,64]{1,0:T(8,128)}, bf16[2,512,768]{2,1,0:T(8,128)(2,1)S...) while((s32[]{:T(128)}, bf16[2,512,4096]{2,1,0:T(8,128)(2,1)}, ...), condition=%wide.wide.region_6.7_spmd, body=%wide.wide.region_5.6_spmd.sunk | while | flops 3229614080 | bytes 11295833 | solution.py:27
  230.0 7.8 %fusion.35 = bf16[2,512,4096]{2,1,0:T(8,128)(2,1)} fusion(bf16[2,512,4096]{2,1,0:T(8,128)(2,1)} %get-tuple-element.131, s32[]{:T(128)} %get-tuple-element.130, bf16[4096,768]{1,0:T(8,128)(2,1)} %get-tuple-element.143, s32[4096]{0:T(1024)S(1)} %get-tuple-element.144, s32[512]{0:T(512)S(1)} %bitcast.77, ...), kind=kOutput, calls=%fused_computation.4.clone.clone.1 | convolution fusion | flops 3229614080 | bytes 11291648 | tf_op jit(solution)/shard_map/while/body/eval_jaxpr/dot_general | solution.py:18
  237.8 7.8 %fusion.35 = bf16[2,512,4096]{2,1,0:T(8,128)(2,1)} fusion(bf16[2,512,4096]{2,1,0:T(8,128)(2,1)} %get-tuple-element.131, s32[]{:T(128)} %get-tuple-element.130, bf16[4096,768]{1,0:T(8,128)(2,1)} %get-tuple-element.143, s32[4096]{0:T(1024)S(1)} %get-tuple-element.144, s32[512]{0:T(512)S(1)} %bitcast.77, ...), kind=kOutput, calls=%fused_computation.4.clone.clone.1 | convolution fusion | flops 3229614080 | bytes 11291648 | tf_op jit(solution)/shard_map/while/body/eval_jaxpr/dot_general | solution.py:18
  245.6 5.8 %convolution_bitcast_fusion = f32[32,4096]{1,0:T(8,128)} fusion(bf16[32,1024]{1,0:T(8,128)(2,1)S(1)} %copy-done, bf16[1024,4096]{1,0:T(8,128)(2,1)} %bitcast.68), kind=kOutput, calls=%fused_computation.9 | convolution fusion | flops 268435456 | bytes 8978432 | tf_op jit(solution)/shard_map/dot_general | solution.py:101
  251.5 0.7 reduce.9
  252.5 28.2 %all-gather.6.cloned.1.call-done = f32[128,4096]{1,0:T(8,128)} async-done(((f32[32,4096]{1,0:T(8,128)}), f32[128,4096]{1,0:T(8,128)}) %all-gather.6.cloned.1.call-update) | async-done | bytes 2097168 | tf_op jit(solution)/shard_map/all_gather | solution.py:101
  280.8 1.7 reduce_sum.49
  282.5 6.6 %fusion.21 = (bf16[32,1024]{1,0:T(8,128)(2,1)S(1)}, f32[32,1024]{1,0:T(8,128)}) fusion(f32[1024]{0:T(1024)S(1)} %select_reduce_fusion, bf16[32,4096]{1,0:T(8,128)(2,1)S(1)} %reduce_sum.49, bf16[1024,4096]{1,0:T(8,128)(2,1)} %bitcast.69), kind=kOutput, calls=%fused_computation.46 | convolution fusion | flops 268500992 | bytes 8851456 | tf_op jit(solution)/shard_map/dot_general | solution.py:104
  289.1 1.1 fusion.7
  290.9 23.3 %reduce-scatter.2.cloned.1.call-done = f32[1,32,768]{2,1,0:T(8,128)} async-done(((f32[4,32,768]{2,1,0:T(8,128)}), f32[1,32,768]{2,1,0:T(8,128)}) %reduce-scatter.2.cloned.1.call-update) | async-done | bytes 98320 | tf_op jit(solution)/shard_map/reduce_scatter | solution.py:117
  314.2 2.2 broadcast_multiply_fusion
  (47 shorter events, 4.6 us)
Async XLA Ops:
  7.2 238.4 %copy-start = (bf16[32,1024]{1,0:T(8,128)(2,1)S(1)}, bf16[32,1024]{1,0:T(8,128)(2,1)}, u32[]{:S(2)}) copy-start(bf16[32,1024]{1,0:T(8,128)(2,1)} %param.13) | copy-start | bytes 196612
  7.2 51.4 %all-gather.4.cloned.1.call-start = ((), (), s32[]{:S(2)}) async-start(), calls=%async_computation.3 | async-start | bytes 1966080 | tf_op jit(solution)/shard_map/all_gather | solution.py:80
  46.4 31.8 %all-to-all-start = ((s32[64,1,64]{2,1,0:T(1,128)}), s32[64,1,64]{2,1,0:T(1,128)S(1)}, u32[]{:S(2)}, u32[]{:S(2)}) async-start(s32[64,1,64]{2,1,0:T(1,128)} %all_to_all.11), calls=%async_computation | async-start | bytes 65536 | tf_op jit(solution)/shard_map/all_to_all | solution.py:95
  78.2 11.9 %copy-start.2 = (s32[64,1,64]{2,1,0:T(1,128)}, s32[64,1,64]{2,1,0:T(1,128)S(1)}, u32[]{:S(2)}) copy-start(s32[64,1,64]{2,1,0:T(1,128)S(1)} %all-to-all-done) | copy-start | bytes 49156
  78.2 11.2 %copy-start.4 = (s32[1,4096]{1,0:T(1,128)S(1)}, s32[1,4096]{1,0:T(1,128)}, u32[]{:S(2)}) copy-start(s32[1,4096]{1,0:T(1,128)} %param.12) | copy-start | bytes 49156
  78.2 151.7 %copy-start.1 = (bf16[1024,768]{1,0:T(8,128)(2,1)S(1)}, bf16[1024,768]{1,0:T(8,128)(2,1)}, u32[]{:S(2)}) copy-start(bf16[1024,768]{1,0:T(8,128)(2,1)} %param.11) | copy-start | bytes 4718596
  78.2 151.7 %all-to-all-start.1 = ((bf16[64,64,768]{2,1,0:T(8,128)(2,1)}), bf16[64,64,768]{2,1,0:T(8,128)(2,1)}, u32[]{:S(2)}, u32[]{:S(2)}) async-start(bf16[64,64,768]{2,1,0:T(8,128)(2,1)} %bitcast.70), calls=%async_computation.1 | async-start | bytes 12582912 | tf_op jit(solution)/shard_map/all_to_all | solution.py:94
  88.8 191.9 %all-gather.6.cloned.1.call-start = ((), (), s32[]{:S(2)}) async-start(), calls=%async_computation.5 | async-start | bytes 2621440 | tf_op jit(solution)/shard_map/all_gather | solution.py:101
  245.6 5.9 %copy-start.3 = (s32[64,64]{1,0:T(8,128)S(1)}, s32[64,64]{1,0:T(8,128)}, u32[]{:S(2)}) copy-start(s32[64,64]{1,0:T(8,128)} %get-tuple-element.161) | copy-start | bytes 49156
  251.4 62.8 %reduce-scatter.2.cloned.1.call-start = ((), (), s32[]{:S(2)}) async-start(), calls=%async_computation.4 | async-start | bytes 491520 | tf_op jit(solution)/shard_map/reduce_scatter | solution.py:117
Sparse Core Ops, SparseCore 0:
  9.8 31.9 all-gather.3
  251.5 29.2 all-gather.5
  290.4 23.7 reduce-scatter.1
